TPU v7x, 512 devices: a whole 4x4x16 slice. The times are simulated.
512 devices in a mesh: fsdp: 8 (over y, x_lo), tensor: 64 (over x_hi, z, core).
Axes of the slice: x: 4 (x_hi: 2, x_lo: 2; x = x_hi * 2 + x_lo), y: 4, z: 16, core: 2. Of those that a mesh axis runs over, the one named last changes fastest.
Arguments:
- tokens: bfloat16 [1024, 8192], P('fsdp', 'tensor'), may hold values from -6 to 6
- in_values: bfloat16 [8192, 3, 8192], P('fsdp', None, 'tensor'), may hold values from -0.1875 to 0.1875
- in_scales: bfloat16 [64, 3, 8192], P('fsdp', None, 'tensor'), may hold values from 0.5 to 2
- filters: float32 [512, 128], P('tensor'), may hold values from -0.6 to 0.6
- out_weight: bfloat16 [8192, 8192], P('tensor', 'fsdp'), may hold values from -0.0625 to 0.0625
- cotangent: bfloat16 [1024, 8192], P('fsdp', 'tensor'), may hold values from -15 to 15
Outputs:
- input_grad: bfloat16 [1024, 8192], P('fsdp', 'tensor')
- filter_grad: float32 [512, 128], P('tensor')
All inputs are finite; a program needn't handle non-finite values.
Results may differ from a plain program's by a relative error of at most 0.012.
Values may be sent and summed in bfloat16 or wider, within the bound.
A program may use at most 128 MiB of HBM per device.

v0:
```python
import jax
import jax.numpy as jnp
from jax import lax
from jax.sharding import PartitionSpec as P

BLOCK = 128


def passed_along(array, axis, by):
    length = lax.axis_size(axis)
    pairs = [(i, i + by) for i in range(length) if 0 <= i + by < length]
    return lax.ppermute(array, axis, pairs)


def dequantize(values, scales):
    blocks = scales.shape[0]
    channels = values.shape[2]
    scaled = (
        values.astype(jnp.float32).reshape(blocks, BLOCK, 3, channels)
        * scales.astype(jnp.float32)[:, None]
    )
    return scaled.reshape(blocks * BLOCK, 3 * channels).astype(jnp.bfloat16)


def apply_taps(filt, extended, rows, per_group, causal):
    taps = filt.shape[1]
    repeated = jnp.repeat(filt, per_group, axis=0)

    def one_step(lag_index, total):
        lag_value = jnp.asarray(lag_index).astype(jnp.int32)
        offset = taps - 1 - lag_value if causal else lag_value
        slab = lax.dynamic_slice_in_dim(extended, offset, rows, 0)
        column = lax.dynamic_slice_in_dim(repeated, lag_value, 1, 1)[:, 0]
        return total + column[None, :] * slab

    return lax.fori_loop(0, taps, one_step, jnp.zeros((rows, repeated.shape[0]), jnp.float32))


def filter_terms(grad_rows, extended, groups_here, per_group, taps):
    rows = grad_rows.shape[0]
    ext_rows = extended.shape[0]
    corr = jnp.einsum(
        "tgj,ugj->gtu",
        grad_rows.reshape(rows, groups_here, per_group),
        extended.reshape(ext_rows, groups_here, per_group),
        precision=lax.Precision.HIGHEST,
    )
    flat = jnp.concatenate(
        [corr.reshape(groups_here, rows * ext_rows), jnp.zeros((groups_here, rows), jnp.float32)], 1
    )
    diagonal = flat.reshape(groups_here, rows, ext_rows + 1)[:, :, :taps]
    return jnp.sum(diagonal, axis=1)[:, ::-1]


def fetch_out(out_weight):
    return lax.all_gather(out_weight, "fsdp", axis=1, tiled=True)


def on_device(tokens, in_values, in_scales, filters, out_weight, cotangent):
    rows = tokens.shape[0]
    channels = tokens.shape[1]
    groups_here, taps = filters.shape
    per_group = channels // groups_here
    whole = lax.all_gather(tokens, "tensor", axis=1, tiled=True)
    values, scales = (
        lax.all_gather(in_values, "fsdp", axis=0, tiled=True),
        lax.all_gather(in_scales, "fsdp", axis=0, tiled=True),
    )
    weight = dequantize(values, scales)
    proj = (
        jnp.dot(whole, weight, preferred_element_type=jnp.float32)
        .astype(jnp.bfloat16)
        .reshape(rows, 3, channels)
    )
    query = proj[:, 0].astype(jnp.float32)
    key_part = proj[:, 1].astype(jnp.float32)
    value_part = proj[:, 2].astype(jnp.float32)
    product = key_part * value_part
    earlier = passed_along(product[rows - (taps - 1) :].astype(jnp.bfloat16), "fsdp", 1).astype(
        jnp.float32
    )
    extended = jnp.concatenate([earlier, product], 0)
    conv = apply_taps(filters, extended, rows, per_group, True)
    out_full = fetch_out(out_weight)
    cot_whole = lax.all_gather(cotangent, "tensor", axis=1, tiled=True)
    grad_z = lax.dot_general(
        cot_whole, out_full, (((1,), (1,)), ((), ())), preferred_element_type=jnp.float32
    )
    grad_query = grad_z * conv
    grad_conv = grad_z * query
    following = passed_along(grad_conv[: taps - 1].astype(jnp.bfloat16), "fsdp", -1).astype(
        jnp.float32
    )
    grad_ext = jnp.concatenate([grad_conv, following], 0)
    grad_product = apply_taps(filters, grad_ext, rows, per_group, False)
    grad_proj = jnp.stack([grad_query, grad_product * value_part, grad_product * key_part], axis=1)
    grad_proj = grad_proj.astype(jnp.bfloat16).reshape(rows, 3 * channels)
    summed = lax.psum_scatter(
        lax.dot_general(
            weight, grad_proj, (((1,), (1,)), ((), ())), preferred_element_type=jnp.float32
        ),
        "tensor",
        scatter_dimension=0,
        tiled=True,
    )
    input_grad = summed.T.astype(jnp.bfloat16)
    local_filter = filter_terms(grad_conv, extended, groups_here, per_group, taps) / rows
    filter_grad = lax.psum(local_filter, "fsdp")
    return (input_grad, filter_grad)


def solution(mesh):
    placed = (
        P("fsdp", "tensor"),
        P("fsdp", None, "tensor"),
        P("fsdp", None, "tensor"),
        P("tensor", None),
        P("tensor", "fsdp"),
        P("fsdp", "tensor"),
    )
    return jax.shard_map(
        on_device,
        mesh=mesh,
        in_specs=placed,
        out_specs=(P("fsdp", "tensor"), P("tensor", None)),
        check_vma=False,
    )
```

profile of v0, /device:TPU:16, one launch (start us, length us, event | category | flops | bytes accessed | tf_op | source)
XLA Modules:
  0.0 812.4 jit_solution(18194216193005715439)
XLA Ops:
  7.2 2.3 copy.16
  9.6 0.7 all-gather.11.cloned.1.call-update
  10.3 0.7 all-gather.9.cloned.1.call-update
  11.7 28.2 %all_gather.16 = bf16[64,3,128]{2,0,1:T(8,128)(2,1)S(1)} all-gather(bf16[8,3,128]{2,0,1:T(8,128)(2,1)} %param.12), channel_id=1, replica_groups=mesh['fsdp'=8,'tensor'=64] {'fsdp'}, dimensions={0}, use_global_device_ids=true | all-gather | bytes 55296 | tf_op jit(solution)/shard_map/all_gather | solution.py:67
  39.9 111.3 %all-gather.5.cloned.1.call-done = bf16[8192,3,128]{0,2,1:T(8,128)(2,1)} async-done(((bf16[1024,3,128]{0,2,1:T(8,128)(2,1)}), bf16[8192,3,128]{0,2,1:T(8,128)(2,1)}) %all-gather.5.cloned.1.call-update) | async-done | bytes 6291472 | tf_op jit(solution)/shard_map/all_gather | solution.py:66
  151.2 7.2 mul.88
  158.4 16.8 %fusion = bf16[8192,384]{0,1:T(8,128)(2,1)} fusion(f32[48,8,64,128]{3,2,1,0:T(8,128)} %bitcast.64, bf16[8192,3,128]{0,2,1:T(8,128)(2,1)} %all-gather.5.cloned.1.call-done), kind=kLoop, calls=%fused_computation.7 | loop fusion | flops 9437184 | bytes 25165824 | tf_op jit(solution)/shard_map/convert_element_type | solution.py:22
  175.2 117.5 %all-gather.11.cloned.1.call-done = bf16[128,8192]{1,0:T(8,128)(2,1)} async-done(((bf16[128,128]{1,0:T(8,128)(2,1)}), bf16[128,8192]{1,0:T(8,128)(2,1)}) %all-gather.11.cloned.1.call-update) | async-done | bytes 2097168 | tf_op jit(solution)/shard_map/all_gather | solution.py:64
  292.6 5.2 convolution_convert_fusion
  297.8 49.0 %all-gather.9.cloned.1.call-done = bf16[128,8192]{1,0:T(8,128)(2,1)} async-done(((bf16[128,1024]{1,0:T(8,128)(2,1)}), bf16[128,8192]{1,0:T(8,128)(2,1)}) %all-gather.9.cloned.1.call-update) | async-done | bytes 2097168 | tf_op jit(solution)/shard_map/all_gather | solution.py:56
  346.9 141.2 %all-gather.7.cloned.1.call-done = bf16[128,8192]{1,0:T(8,128)(2,1)} async-done(((bf16[128,128]{1,0:T(8,128)(2,1)}), bf16[128,8192]{1,0:T(8,128)(2,1)}) %all-gather.7.cloned.1.call-update) | async-done | bytes 2097168 | tf_op jit(solution)/shard_map/all_gather | solution.py:85
  488.1 2.9 convert_multiply_fusion.1
  491.1 2.7 collective-permute-start
  493.8 13.8 %mul.89 = f32[8192,3,128]{0,2,1:T(8,128)} reshape(f32[64,128,3,128]{1,0,3,2:T(8,128)} %mul.88) | data formatting | bytes 25165824 | tf_op jit(solution)/shard_map/mul | solution.py:19
  507.8 4.3 collective-permute-start.1
  512.1 33.2 %while.30 = (s32[]{:T(128)}, f32[128,128]{1,0:T(8,128)S(1)}, f32[128,128]{0,1:T(8,128)S(1)}, f32[255,128]{0,1:T(8,128)S(1)}, s32[]{:T(128)}, /*index=5*/s32[]{:T(128)}, s32[]{:T(128)}, s32[]{:T(128)}) while((s32[]{:T(128)}, f32[128,128]{1,0:T(8,128)S(1)}, f32[128,128]{0,1:T(8,128)S(1)}, f32[255,128]{0,1:T(8,128)S(1)}, s32[]{:T(128)}, ...), condition=%wide.region_1.0_spmd.clone, body=%wide.region_0.0_spmd.clone.sunk | while | flops 49159 | bytes 460437 | solution.py:36
  545.5 32.5 %while.31 = (s32[]{:T(128)}, f32[128,128]{1,0:T(8,128)S(1)}, f32[128,128]{0,1:T(8,128)S(1)}, f32[255,128]{0,1:T(8,128)S(1)}, s32[]{:T(128)}, /*index=5*/s32[]{:T(128)}) while((s32[]{:T(128)}, f32[128,128]{1,0:T(8,128)S(1)}, f32[128,128]{0,1:T(8,128)S(1)}, f32[255,128]{0,1:T(8,128)S(1)}, s32[]{:T(128)}, /*index=5*/s32[]{:T(128)}) %tuple.96), condition=%wide.region_3.0_spmd.clone, body=%wide.region_2.0_spmd.clone.sunk | while | flops 49155 | bytes 460375 | solution.py:36
  578.2 10.5 %convolution_bitcast_fusion = f32[8192,128]{1,0:T(8,128)} fusion(f32[8192,3,128]{0,2,1:T(8,128)} %mul.89, bf16[8192,3,128]{0,2,1:T(8,128)(2,1)} %all-gather.5.cloned.1.call-done, bf16[128,1,128]{0,2,1:T(8,128)(2,1)S(1)} %get-tuple-element.260, bf16[128,1,128]{0,2,1:T(8,128)(2,1)S(1)} %get-tuple-element.259, bf16[128,1,128]{0,2,1:T(8,128)(2,1)S(1)} %fusion.9), kind=kOutput, calls=%fused_computation.9 | convolution fusion | flops 814841856 | bytes 23166976 | tf_op jit(solution)/shard_map/dot_general | solution.py:99
  588.7 1.0 fusion.13
  589.8 0.6 reshape.48
  590.7 14.2 %psum.7 = f32[8,128]{1,0:T(8,128)} all-reduce(f32[8,128]{1,0:T(8,128)S(1)} %broadcast_multiply_fusion), channel_id=1, replica_groups=mesh['fsdp'=8,'tensor'=64] {'fsdp'}, use_global_device_ids=true, to_apply=%region_6.0 | all-reduce | flops 1024 | bytes 8192 | tf_op jit(solution)/shard_map/psum | solution.py:108
  604.8 199.5 %reduce-scatter.2.cloned.1.call-done = f32[128,128]{1,0:T(8,128)} async-done(((f32[8192,128]{1,0:T(8,128)}), f32[128,128]{1,0:T(8,128)}) %reduce-scatter.2.cloned.1.call-update) | async-done | bytes 65552 | tf_op jit(solution)/shard_map/reduce_scatter | solution.py:98
  804.3 0.8 convert_bitcast_fusion
  805.2 0.7 copy.27
  (1055 shorter events, 54.7 us)
Async XLA Ops:
  7.2 144.1 %all-gather.5.cloned.1.call-start = ((), (), s32[]{:S(2)}) async-start(), calls=%async_computation.1 | async-start | bytes 7077888 | tf_op jit(solution)/shard_map/all_gather | solution.py:66
  9.5 283.1 %all-gather.11.cloned.1.call-start = ((), (), s32[]{:S(2)}) async-start(), calls=%async_computation.4 | async-start | bytes 2129920 | tf_op jit(solution)/shard_map/all_gather | solution.py:64
  10.3 336.6 %all-gather.9.cloned.1.call-start = ((), (), s32[]{:S(2)}) async-start(), calls=%async_computation.3 | async-start | bytes 2359296 | tf_op jit(solution)/shard_map/all_gather | solution.py:56
  11.0 477.1 %all-gather.7.cloned.1.call-start = ((), (), s32[]{:S(2)}) async-start(), calls=%async_computation.2 | async-start | bytes 2129920 | tf_op jit(solution)/shard_map/all_gather | solution.py:85
  11.6 792.7 %reduce-scatter.2.cloned.1.call-start = ((), (), s32[]{:S(2)}) async-start(), calls=%async_computation.5 | async-start | bytes 4259840 | tf_op jit(solution)/shard_map/reduce_scatter | solution.py:98
  491.1 20.9 %collective-permute-start = (bf16[127,128]{0,1:T(8,128)(2,1)S(1)}, bf16[127,128]{0,1:T(8,128)(2,1)S(1)}, u32[]{:S(2)}, u32[]{:S(2)}) collective-permute-start(bf16[127,128]{0,1:T(8,128)(2,1)S(1)} %slice.49), channel_id=1, source_target_pairs={{0,64},{64,128},{128,192},{192,256},{256,320},{320,384},{384,448},... | collective-permute-start | bytes 97544 | tf_op jit(solution)/shard_map/ppermute | solution.py:12
  493.8 13.8 %copy-start = (f32[8,128]{1,0:T(8,128)S(1)}, f32[8,128]{1,0:T(8,128)}, u32[]{:S(2)}) copy-start(f32[8,128]{1,0:T(8,128)} %param.13) | copy-start | bytes 12292
  507.8 37.7 %collective-permute-start.1 = (bf16[127,128]{0,1:T(8,128)(2,1)S(1)}, bf16[127,128]{0,1:T(8,128)(2,1)S(1)}, u32[]{:S(2)}, u32[]{:S(2)}) collective-permute-start(bf16[127,128]{0,1:T(8,128)(2,1)S(1)} %slice.48), channel_id=1, source_target_pairs={{64,0},{128,64},{192,128},{256,192},{320,256},{384,320},{448,384},... | collective-permute-start | bytes 97544 | tf_op jit(solution)/shard_map/ppermute | solution.py:12
Sparse Core Ops, SparseCore 0:
  10.1 141.1 all-gather.4
  154.2 138.3 all-gather.10
  294.7 52.1 all-gather.8
  349.7 138.3 all-gather.6
  588.8 215.4 reduce-scatter.1
where the time goes:
time: 813 us; the launch traced here: 812 us
  waiting for transfers between devices  620 us (76%)
  local copies, waits for them, and re-layouts  73.6 us (9%)
  blocking collectives  42.4 us (5%)
  other arithmetic  22.5 us (3%)
  matrix products  19.7 us (2%)
  between operations  14 us (2%)
  loops' own time  12.7 us (2%)
    reduce_scatter x1, waiting for transfers between devices, on_device(): lax.psum_scatter(lax.dot_general(weight, grad_proj, (((1,), (1,)), ((), (...  199 us
    all_gather x1, waiting for transfers between devices, on_device(): cot_whole = lax.all_gather(cotangent, 'tensor', axis=1, tiled=True)  141 us
    all_gather x1, waiting for transfers between devices, on_device(): whole = lax.all_gather(tokens, 'tensor', axis=1, tiled=True)  117 us
    all_gather x1, waiting for transfers between devices, on_device(): lax.all_gather(in_values, 'fsdp', axis=0, tiled=True)  111 us
    all_gather x1, waiting for transfers between devices, fetch_out(): return lax.all_gather(out_weight, 'fsdp', axis=1, tiled=True)  49 us
    dynamic_slice x512, local copies, waits for them, and re-layouts, one_step(): slab = lax.dynamic_slice_in_dim(extended, offset, rows, 0)  45.3 us
    all_gather x1, blocking collectives, on_device(): lax.all_gather(in_scales, 'fsdp', axis=0, tiled=True)  28.2 us
    mul x2, local copies, waits for them, and re-layouts, dequantize(): values.astype(jnp.float32).reshape(blocks, BLOCK, 3, channels)  21 us
  transfers between devices with their start and end apart: 7, of which 5 were waited for; matrix products, arithmetic and copies ran while one was open for 9% of the time, Pallas kernels for 0%

commit v1 on v0

v1 whole, which is shorter than its diff:
```python
import functools

import jax
import jax.numpy as jnp
from jax import lax
from jax.experimental import pallas as pl
from jax.experimental.pallas import tpu as pltpu
from jax.sharding import PartitionSpec as P

MESH = pl.DeviceIdType.MESH
BLOCK = 128
GROUP = 16
PIECES = 8
UP, DOWN = 0, 1


def piece_at(position):
    odd_node, core, half = position // 4, (position // 2) % 2, position % 2
    return 4 * odd_node + 2 * half + 1 - core


def dot(a, b, contract, precision=None):
    return lax.dot_general(
        a, b, ((contract[:1], contract[1:]), ((), ())),
        preferred_element_type=jnp.float32, precision=precision,
    )


def exact(a, b, contract):
    return dot(a, b, contract, lax.Precision.HIGHEST)


def kernel(
    n_f, n_z,
    tok, cot, val, scl, flt, out_w,
    input_grad, filter_grad,
    tok_all, cot_all, wt, wn, ow, part, gz_part, part_in, gz_in, gp, fg_all,
    own, pair_out, pair_in, ring_out, ring_in, last_out, last_in,
    perm_s, perm_r, ring_s, ring_r, core_s, core_r, rs_s, rs_r, ag_s, ag_r, fg_s, fg_r,
    pair_s, pair_r, sum_s, sum_r, last_s, last_r,
):
    channels = val.shape[2]
    f, m = lax.axis_index("fsdp"), lax.axis_index("tensor")
    c, z, xh = lax.rem(m, 2), lax.rem(m // 2, n_z), m // (2 * n_z)
    along = lambda by: lax.rem(z + by + 2 * n_z, n_z)
    up = (xh * n_z + along(1)) * 2 + c
    down = (xh * n_z + along(-1)) * 2 + c
    other = m + 1 - 2 * c
    peer = lambda k: lax.rem(f + k, n_f)

    jm = lax.rem(m, PIECES)
    to_f, to_z, to_c, to_half = m // PIECES, 2 * f + jm // 4, 1 - lax.rem(jm, 2), lax.rem(jm, 4) // 2
    to_m = lambda x: (x * n_z + to_z) * 2 + to_c
    from_f = z // 2
    from_m = lambda half: PIECES * f + 4 * lax.rem(z, 2) + 2 * half + 1 - c

    def remote(src, dst, send, recv, fsdp, tensor):
        return pltpu.make_async_remote_copy(
            src_ref=src, dst_ref=dst, send_sem=send, recv_sem=recv,
            device_id={"fsdp": fsdp, "tensor": tensor}, device_id_type=MESH,
        )

    sent = []

    def start(copy):
        copy.start()
        sent.append(copy)

    barrier = pltpu.get_barrier_semaphore()
    greeted = [(f, up), (f, down), (f, other)]
    greeted += [(peer(k), m) for k in range(1, n_f)]
    greeted += [(to_f, to_m(x)) for x in range(2)]
    greeted += [(from_f, from_m(h)) for h in range(2)]
    for fsdp, tensor in greeted:
        pl.semaphore_signal(
            barrier, inc=1, device_id={"fsdp": fsdp, "tensor": tensor}, device_id_type=MESH
        )
    pl.semaphore_wait(barrier, len(greeted))

    gathered = (tok_all, cot_all)
    for a, block in enumerate((tok, cot)):
        for x in range(2):
            start(remote(
                block, gathered[a].at[to_z, to_c, to_half],
                perm_s.at[a, x], perm_r.at[a, to_half], to_f, to_m(x),
            ))

    for position in range(PIECES):
        piece = piece_at(position)
        rows = slice(position * BLOCK, (position + 1) * BLOCK)
        for j in range(3):
            scaled = val[j, piece * BLOCK : (piece + 1) * BLOCK, :].astype(jnp.float32) * scl[
                j, piece : piece + 1, :
            ].astype(jnp.float32)
            columns = slice(j * channels, (j + 1) * channels)
            wn[rows, columns] = scaled.astype(jnp.bfloat16)
            wt[columns, rows] = scaled.T.astype(jnp.bfloat16)
        ow[:, rows] = out_w[:, piece * BLOCK : (piece + 1) * BLOCK]

    steps = ((n_z // 2, n_z // 2 - 1), (n_z // 2 - 1, n_z // 2))

    def ring(a, way, step):
        slot = along(-step if way == UP else step)
        chunk = gathered[a].at[slot, c]
        return remote(
            chunk, chunk, ring_s.at[a, way, step], ring_r.at[a, way, step],
            f, up if way == UP else down,
        )

    def landed(a, way, step):
        slot = along(-step - 1 if way == UP else step + 1)
        chunk = gathered[a].at[slot, c]
        return remote(
            chunk, chunk, ring_s.at[a, way, step], ring_r.at[a, way, step],
            f, up if way == UP else down,
        )

    def order(a):
        return [(0, 0)] + [(1 + s, -s - 1) for s in range(steps[a][UP])] + [
            (1 + steps[a][UP] + s, s + 1) for s in range(steps[a][DOWN])
        ]

    def across(a, index, by, core):
        chunk = gathered[a].at[along(by), core]
        return remote(chunk, chunk, core_s.at[a, index], core_r.at[a, index], f, other)

    for a in range(2):
        for half in range(2):
            block = gathered[a].at[z, c, half]
            remote(block, block, perm_s.at[a, half], perm_r.at[a, half], f, other).wait_recv()
        for way in (UP, DOWN):
            start(ring(a, way, 0))
        start(across(a, 0, 0, c))
    for step in range(n_z // 2):
        for a in range(2):
            for way in (UP, DOWN):
                if step < steps[a][way]:
                    landed(a, way, step).wait_recv()
                    if step + 1 < steps[a][way]:
                        start(ring(a, way, step + 1))
                    if way == UP:
                        start(across(a, 1 + step, -step - 1, c))
                    else:
                        start(across(a, 1 + steps[a][UP] + step, step + 1, c))
    for a in range(2):
        for index, by in order(a):
            across(a, index, by, 1 - c).wait_recv()

    def gathered_rows(buffer, tb):
        blocks = [buffer[2 * tb + n, core, half] for n in range(2) for core in range(2) for half in range(2)]
        return jnp.concatenate(blocks, axis=1)

    def forward(tb, carry):
        columns = pl.ds(pl.multiple_of(tb * BLOCK, BLOCK), BLOCK)
        proj = dot(wt[...], gathered_rows(tok_all, tb), (1, 1)).astype(jnp.bfloat16)
        for j in range(3):
            part[j, :, columns] = proj[j * channels : (j + 1) * channels]
        gz_part[:, columns] = dot(ow[...], gathered_rows(cot_all, tb), (1, 1)).astype(jnp.bfloat16)
        return carry

    lax.fori_loop(0, n_f, forward, 0)

    group_rows = lambda g: pl.ds(pl.multiple_of(g * GROUP, GROUP), GROUP)

    def scatter(k):
        return (
            remote(part.at[:, group_rows(peer(k)), :], part_in.at[k - 1], rs_s.at[0, k - 1], rs_r.at[0, k - 1], peer(k), m),
            remote(gz_part.at[group_rows(peer(k)), :], gz_in.at[k - 1], rs_s.at[1, k - 1], rs_r.at[1, k - 1], peer(k), m),
        )

    for k in range(1, n_f):
        for copy in scatter(k):
            start(copy)
    mine = group_rows(f)
    proj_sum = part[:, mine, :].astype(jnp.float32)
    gz_sum = gz_part[mine, :].astype(jnp.float32)
    for k in range(1, n_f):
        for copy in scatter(k):
            copy.wait_recv()
        proj_sum = proj_sum + part_in[k - 1].astype(jnp.float32)
        gz_sum = gz_sum + gz_in[k - 1].astype(jnp.float32)

    def stacked(x):
        return jnp.concatenate([x[:, b * BLOCK : (b + 1) * BLOCK] for b in range(n_f)], axis=0)

    def unstacked(x):
        return jnp.concatenate([x[b * GROUP : (b + 1) * GROUP] for b in range(n_f)], axis=1)

    proj_sum = proj_sum.astype(jnp.bfloat16).astype(jnp.float32)
    query, key, value = (stacked(proj_sum[j]) for j in range(3))
    grad_z = stacked(gz_sum)
    nothing = jnp.zeros((GROUP, BLOCK), jnp.float32)
    product = key * value
    before = jnp.concatenate([nothing, product[:-GROUP]], axis=0)
    taps = jnp.concatenate([flt[pl.ds(f, 1), :], jnp.zeros((1, BLOCK), jnp.float32)], axis=1)
    band = pltpu.roll(jnp.broadcast_to(taps, (BLOCK, 2 * BLOCK)), 0, 1, stride=1, stride_axis=0)
    band_here, band_next = band[:, :BLOCK], band[:, BLOCK:]
    conv = exact(product, band_here, (1, 0)) + exact(before, band_next, (1, 0))
    grad_query = grad_z * conv
    grad_conv = grad_z * query
    after = jnp.concatenate([grad_conv[GROUP:], nothing], axis=0)
    grad_product = exact(grad_conv, band_here, (1, 1)) + exact(after, band_next, (1, 1))
    for j, grad in enumerate((grad_query, grad_product * value, grad_product * key)):
        gp[j, mine, :] = unstacked(grad).astype(jnp.bfloat16)

    def share(k, owner):
        rows = gp.at[:, group_rows(owner), :]
        return remote(rows, rows, ag_s.at[k - 1], ag_r.at[k - 1], peer(k), m)

    for k in range(1, n_f):
        start(share(k, f))

    flip = (
        lax.broadcasted_iota(jnp.int32, (BLOCK, BLOCK), 0)
        + lax.broadcasted_iota(jnp.int32, (BLOCK, BLOCK), 1)
        == BLOCK - 1
    ).astype(jnp.float32)
    turned = exact(product, flip, (1, 0))
    corr = exact(turned, jnp.concatenate([grad_conv, after], axis=1), (0, 0))
    skewed = pltpu.roll(corr, 0, 1, stride=1, stride_axis=0)
    lags = pltpu.roll(jnp.sum(skewed, axis=0, keepdims=True), BLOCK + 1, 1)[:, :BLOCK]
    fg_all[f] = jnp.broadcast_to(lags * (1.0 / BLOCK), (8, BLOCK))

    def share_filter(k, owner):
        return remote(fg_all.at[owner], fg_all.at[owner], fg_s.at[k - 1], fg_r.at[k - 1], peer(k), m)

    for k in range(1, n_f):
        start(share_filter(k, f))
    for k in range(1, n_f):
        share(k, peer(n_f - k)).wait_recv()

    wide = 2 * BLOCK

    def backward(i, core):
        columns = pl.ds(pl.multiple_of(i * wide, wide), wide)
        grads = jnp.concatenate([gp[j, :, columns] for j in range(3)], axis=0)
        return [
            dot(wn[pl.ds(pl.multiple_of((4 * n + 2 * core) * BLOCK, wide), wide), :], grads, (1, 0))
            for n in range(2)
        ]

    def pair(i):
        chunks = pl.ds(4 * i, 4)
        return remote(pair_out.at[chunks], pair_in.at[chunks], pair_s.at[i], pair_r.at[i], f, other)

    for i in range(n_f // 2):
        halves = backward(i, 1 - c)
        for t in range(2):
            for n in range(2):
                pair_out[4 * i + 2 * t + n] = halves[n][:, t * BLOCK : (t + 1) * BLOCK].astype(jnp.bfloat16)
        start(pair(i))
    for i in range(n_f // 2):
        halves = backward(i, c)
        for t in range(2):
            for n in range(2):
                own[4 * i + 2 * t + n] = halves[n][:, t * BLOCK : (t + 1) * BLOCK]
    for i in range(n_f // 2):
        pair(i).wait_recv()

    hops = (n_z // 2, n_z // 2 - 1)

    def pass_on(way, step):
        return remote(
            ring_out.at[way, step], ring_in.at[way, step], sum_s.at[way, step], sum_r.at[way, step],
            f, up if way == UP else down,
        )

    for step in range(n_z // 2):
        for way in (UP, DOWN):
            if step < hops[way]:
                slot = along(hops[UP] - step if way == UP else step - hops[DOWN])
                total = own[slot] + pair_in[slot].astype(jnp.float32)
                if step > 0:
                    pass_on(way, step - 1).wait_recv()
                    total = total + ring_in[way, step - 1].astype(jnp.float32)
                ring_out[way, step] = total.astype(jnp.bfloat16)
                start(pass_on(way, step))
    total = own[z] + pair_in[z].astype(jnp.float32)
    for way in (UP, DOWN):
        pass_on(way, hops[way] - 1).wait_recv()
        total = total + ring_in[way, hops[way] - 1].astype(jnp.float32)

    for half in range(2):
        last_out[half] = total[half * BLOCK : (half + 1) * BLOCK].astype(jnp.bfloat16)
        start(remote(
            last_out.at[half], last_in.at[xh], last_s.at[half], last_r.at[xh], from_f, from_m(half)
        ))
    for x in range(2):
        remote(last_out.at[x], last_in.at[x], last_s.at[x], last_r.at[x], to_f, to_m(x)).wait_recv()
    summed = last_in[0].astype(jnp.float32) + last_in[1].astype(jnp.float32)
    input_grad[...] = summed.T.astype(jnp.bfloat16)

    for k in range(1, n_f):
        share_filter(k, peer(n_f - k)).wait_recv()
    filter_grad[...] = jnp.concatenate([fg_all[g, 0:1, :] for g in range(n_f)], axis=0)
    for copy in sent:
        copy.wait_send()


def on_device(n_f, n_z, tokens, in_values, in_scales, filters, out_weight, cotangent):
    channels = in_values.shape[2]
    features = PIECES * BLOCK
    length = n_f * BLOCK
    bf16, f32 = jnp.bfloat16, jnp.float32
    dma = pltpu.SemaphoreType.DMA
    return pl.pallas_call(
        functools.partial(kernel, n_f, n_z),
        out_shape=(
            jax.ShapeDtypeStruct((BLOCK, BLOCK), bf16),
            jax.ShapeDtypeStruct((n_f, BLOCK), f32),
        ),
        in_specs=[pl.BlockSpec(memory_space=pltpu.VMEM)] * 6,
        out_specs=(pl.BlockSpec(memory_space=pltpu.VMEM),) * 2,
        scratch_shapes=[
            pltpu.VMEM((n_z, 2, 2, BLOCK, BLOCK), bf16),
            pltpu.VMEM((n_z, 2, 2, BLOCK, BLOCK), bf16),
            pltpu.VMEM((3 * channels, features), bf16),
            pltpu.VMEM((features, 3 * channels), bf16),
            pltpu.VMEM((channels, features), bf16),
            pltpu.VMEM((3, channels, length), bf16),
            pltpu.VMEM((channels, length), bf16),
            pltpu.VMEM((n_f - 1, 3, GROUP, length), bf16),
            pltpu.VMEM((n_f - 1, GROUP, length), bf16),
            pltpu.VMEM((3, channels, length), bf16),
            pltpu.VMEM((n_f, 8, BLOCK), f32),
            pltpu.VMEM((n_z, 2 * BLOCK, BLOCK), f32),
            pltpu.VMEM((n_z, 2 * BLOCK, BLOCK), bf16),
            pltpu.VMEM((n_z, 2 * BLOCK, BLOCK), bf16),
            pltpu.VMEM((2, n_z // 2, 2 * BLOCK, BLOCK), bf16),
            pltpu.VMEM((2, n_z // 2, 2 * BLOCK, BLOCK), bf16),
            pltpu.VMEM((2, BLOCK, BLOCK), bf16),
            pltpu.VMEM((2, BLOCK, BLOCK), bf16),
            dma((2, 2)), dma((2, 2)),
            dma((2, 2, n_z // 2)), dma((2, 2, n_z // 2)),
            dma((2, n_z)), dma((2, n_z)),
            dma((2, n_f - 1)), dma((2, n_f - 1)),
            dma((n_f - 1,)), dma((n_f - 1,)),
            dma((n_f - 1,)), dma((n_f - 1,)),
            dma((n_f // 2,)), dma((n_f // 2,)),
            dma((2, n_z // 2)), dma((2, n_z // 2)),
            dma((2,)), dma((2,)),
        ],
        compiler_params=pltpu.CompilerParams(
            collective_id=0, has_side_effects=True, vmem_limit_bytes=48 << 20
        ),
        name="hyena",
    )(
        tokens, cotangent, in_values.transpose(1, 0, 2), in_scales.transpose(1, 0, 2),
        filters, out_weight,
    )


def solution(mesh):
    placed = (
        P("fsdp", "tensor"),
        P("fsdp", None, "tensor"),
        P("fsdp", None, "tensor"),
        P("tensor", None),
        P("tensor", "fsdp"),
        P("fsdp", "tensor"),
    )
    return jax.shard_map(
        functools.partial(on_device, mesh.shape["fsdp"], mesh.shape["tensor"] // 4),
        mesh=mesh,
        in_specs=placed,
        out_specs=(P("fsdp", "tensor"), P("tensor", None)),
        check_vma=False,
    )
```

time: 813 us -> 152 us (0.19)
  the two profiles are of different devices: /device:TPU:16 before, /device:TPU:17 now
where the time goes in v1:
time: 152 us; the launch traced here: 151 us
  Pallas kernels  144 us (95%)
  local copies, waits for them, and re-layouts  6.18 us (4%)
    pallas_call x1, Pallas kernels, on_device(): pl.pallas_call(functools.partial(kernel, n_f, n_z), out_shape=(jax.ShapeD...  144 us
    unnamed x14, local copies, waits for them, and re-layouts  6.18 us

profile of v1, /device:TPU:17, one launch (start us, length us, event | category | flops | bytes accessed | tf_op | source)
XLA Modules:
  0.0 151.3 jit_solution(11252248671741076324)
XLA Ops:
  0.6 0.0 copy-start
  0.6 1.1 copy-done
  1.8 0.0 copy-start.1
  1.8 0.9 copy-done.1
  2.7 0.0 copy-start.2
  2.7 0.8 copy-done.2
  3.5 0.0 copy-start.3
  3.5 0.8 copy-done.3
  4.2 0.0 copy-start.4
  4.2 0.7 copy-done.4
  4.9 0.0 copy-start.5
  4.9 0.7 copy-done.5
  5.6 144.5 %hyena.1 = (bf16[128,128]{1,0:T(8,128)(2,1)S(1)}, f32[8,128]{1,0:T(8,128)S(1)}) custom-call(bf16[128,128]{1,0:T(8,128)(2,1)S(1)} %copy-done.2, bf16[128,128]{1,0:T(8,128)(2,1)S(1)} %copy-done.3, bf16[3,1024,128]{2,1,0:T(8,128)(2,1)S(1)} %bitcast.2, bf16[3,8,128]{2,1,0:T(8,128)(2,1)S(1)} %bitcast.3, f32[8,128]{1,0:T(8,128)S(1)} %copy-done.5, ...), custom_call_target="tpu_custom_call" | custom-call | tf_op jit(solution)/shard_map/hyena/pallas_call | solution.py:306
  150.1 0.6 copy.10
  150.7 0.6 copy.11
Async XLA Ops:
  0.6 1.1 copy-start
  1.8 0.9 copy-start.1
  2.7 0.8 copy-start.2
  3.5 0.8 copy-start.3
  4.2 0.7 copy-start.4
  4.9 0.7 copy-start.5

commit v2 on v1

v2 whole, which is shorter than its diff:
```python
import functools

import jax
import jax.numpy as jnp
from jax import lax
from jax.experimental import pallas as pl
from jax.experimental.pallas import tpu as pltpu
from jax.sharding import PartitionSpec as P

MESH = pl.DeviceIdType.MESH
BLOCK = 128
GROUP = 16
PIECES = 8
UP, DOWN = 0, 1


def piece_at(position):
    odd_node, core, half = position // 4, (position // 2) % 2, position % 2
    return 4 * odd_node + 2 * half + 1 - core


def dot(a, b, contract, precision=None):
    return lax.dot_general(
        a, b, ((contract[:1], contract[1:]), ((), ())),
        preferred_element_type=jnp.float32, precision=precision,
    )


def exact(a, b, contract):
    return dot(a, b, contract, lax.Precision.HIGHEST)


def kernel(
    n_f, n_z,
    tok, cot, val_hbm, scl_hbm, flt_hbm, out_w_hbm,
    input_grad, filter_grad,
    val, scl, flt, out_w, gathered, wt, wn, ow, part, part_in, gp, fg_all,
    own, pair_out, pair_in, ring_out, ring_in, last_out, last_in,
    in_s, perm_s, perm_r, ring_s, ring_r, slice_s, slice_r, core_s, core_r, rs_s, rs_r, ag_s, ag_r, fg_s, fg_r,
    pair_s, pair_r, sum_s, sum_r, last_s, last_r,
):
    channels = val.shape[2]
    half_z, half_f = n_z // 2, n_f // 2
    f, m = lax.axis_index("fsdp"), lax.axis_index("tensor")
    c, z, xh = lax.rem(m, 2), lax.rem(m // 2, n_z), m // (2 * n_z)
    along = lambda by: lax.rem(z + by + 2 * n_z, n_z)
    up = (xh * n_z + along(1)) * 2 + c
    down = (xh * n_z + along(-1)) * 2 + c
    other = m + 1 - 2 * c
    across_x = ((1 - xh) * n_z + z) * 2 + c
    peer = lambda k: lax.rem(f + k, n_f)
    tokens_at = lambda off: lax.rem(z // 2 + off + n_f, n_f)

    jm = lax.rem(m, PIECES)
    to_f, to_z, to_c, to_half = m // PIECES, 2 * f + jm // 4, 1 - lax.rem(jm, 2), lax.rem(jm, 4) // 2
    to_m = lambda x: (x * n_z + to_z) * 2 + to_c
    from_f = z // 2
    from_m = lambda half: PIECES * f + 4 * lax.rem(z, 2) + 2 * half + 1 - c

    def remote(src, dst, send, recv, fsdp, tensor):
        return pltpu.make_async_remote_copy(
            src_ref=src, dst_ref=dst, send_sem=send, recv_sem=recv,
            device_id={"fsdp": fsdp, "tensor": tensor}, device_id_type=MESH,
        )

    sent = []

    def start(copy):
        copy.start()
        sent.append(copy)

    loads = [
        pltpu.make_async_copy(src, dst, in_s.at[i])
        for i, (src, dst) in enumerate(
            ((val_hbm, val), (scl_hbm, scl), (flt_hbm, flt), (out_w_hbm, out_w))
        )
    ]
    for load in loads:
        load.start()
    barrier = pltpu.get_barrier_semaphore()
    greeted = [(f, up), (f, down), (f, other), (f, across_x)]
    greeted += [(peer(k), m) for k in range(1, n_f)]
    greeted += [(to_f, to_m(x)) for x in range(2)]
    greeted += [(from_f, from_m(h)) for h in range(2)]
    for fsdp, tensor in greeted:
        pl.semaphore_signal(
            barrier, inc=1, device_id={"fsdp": fsdp, "tensor": tensor}, device_id_type=MESH
        )
    pl.semaphore_wait(barrier, len(greeted))

    for a, block in enumerate((tok, cot)):
        start(remote(
            block, gathered.at[to_z, to_c, to_half, a], perm_s.at[a], perm_r.at[a], to_f, to_m(to_half)
        ))

    for load in loads:
        load.wait()
    for position in range(PIECES):
        piece = piece_at(position)
        rows = slice(position * BLOCK, (position + 1) * BLOCK)
        for j in range(3):
            scaled = val[j, piece * BLOCK : (piece + 1) * BLOCK, :].astype(jnp.float32) * scl[
                j, piece : piece + 1, :
            ].astype(jnp.float32)
            columns = slice(j * channels, (j + 1) * channels)
            wn[rows, columns] = scaled.astype(jnp.bfloat16)
            wt[columns, rows] = scaled.T.astype(jnp.bfloat16)
        ow[:, rows] = out_w[:, piece * BLOCK : (piece + 1) * BLOCK]

    steps = ((half_z, half_z - 1), (half_z - 1, half_z))

    def ring(a, way, step, ahead=0):
        slot = along(-step - ahead if way == UP else step + ahead)
        chunk = gathered.at[slot, c, xh, a]
        return remote(
            chunk, chunk, ring_s.at[a, way, step], ring_r.at[a, way, step],
            f, up if way == UP else down,
        )

    def over_x(by, half):
        chunk = gathered.at[along(by), c, half]
        return remote(chunk, chunk, slice_s.at[by % n_z], slice_r.at[by % n_z], f, across_x)

    def over_core(by, half, which, core):
        chunk = gathered.at[along(by), core, half]
        return remote(chunk, chunk, core_s.at[which, by % n_z], core_r.at[which, by % n_z], f, other)

    def nodes_at(distance):
        return [distance] if distance in (0, half_z) else [-distance, distance]

    def rows_of(tb, a):
        blocks = [gathered[2 * tb + n, core, half, a] for n in range(2) for core in range(2) for half in range(2)]
        return jnp.concatenate(blocks, axis=1)

    group_rows = lambda g: pl.ds(pl.multiple_of(g * GROUP, GROUP), GROUP)

    def scatter(k, off):
        return remote(
            part.at[tokens_at(off), :, group_rows(peer(k)), :], part_in.at[k - 1, tokens_at(off)],
            rs_s.at[k - 1, off % n_f], rs_r.at[k - 1, off % n_f], peer(k), m,
        )

    def products(distance):
        for d in (2 * distance, 2 * distance + 1):
            if d <= half_z:
                for by in nodes_at(d):
                    over_core(by, xh, 0, 1 - c).wait_recv()
                    over_core(by, 1 - xh, 1, 1 - c).wait_recv()
        for off in [distance] if distance in (0, half_f) else [-distance, distance]:
            tb = tokens_at(off)
            proj = dot(wt[...], rows_of(tb, 0), (1, 1)).astype(jnp.bfloat16)
            for j in range(3):
                part[tb, j] = proj[j * channels : (j + 1) * channels]
            part[tb, 3] = dot(ow[...], rows_of(tb, 1), (1, 1)).astype(jnp.bfloat16)
            for k in range(1, n_f):
                start(scatter(k, off))

    for a in range(2):
        block = gathered.at[z, c, xh, a]
        remote(block, block, perm_s.at[a], perm_r.at[a], f, other).wait_recv()
        for way in (UP, DOWN):
            start(ring(a, way, 0))
    start(over_x(0, xh))
    start(over_core(0, xh, 0, c))
    done = 0
    for step in range(half_z):
        for a in range(2):
            for way in (UP, DOWN):
                if step < steps[a][way]:
                    ring(a, way, step, 1).wait_recv()
                    if step + 1 < steps[a][way]:
                        start(ring(a, way, step + 1))
        for by in nodes_at(step + 1):
            start(over_x(by, xh))
            start(over_core(by, xh, 0, c))
        for by in nodes_at(step):
            over_x(by, 1 - xh).wait_recv()
            start(over_core(by, 1 - xh, 1, c))
        if step == 2 * done + 2:
            products(done)
            done += 1
    for by in nodes_at(half_z):
        over_x(by, 1 - xh).wait_recv()
        start(over_core(by, 1 - xh, 1, c))
    for distance in range(done, half_f + 1):
        products(distance)

    mine = group_rows(f)
    offsets = [off for d in range(half_f + 1) for off in ([d] if d in (0, half_f) else [-d, d])]
    taps = jnp.concatenate([flt[pl.ds(f, 1), :], jnp.zeros((1, BLOCK), jnp.float32)], axis=1)
    band = pltpu.roll(jnp.broadcast_to(taps, (BLOCK, 2 * BLOCK)), 0, 1, stride=1, stride_axis=0)
    band_here, band_next = band[:, :BLOCK], band[:, BLOCK:]
    for off in offsets:
        for k in range(1, n_f):
            scatter(k, off).wait_recv()

    def summed_part(j):
        total = part[:, j, mine, :].astype(jnp.float32)
        for k in range(1, n_f):
            total = total + part_in[k - 1, :, j].astype(jnp.float32)
        return total.reshape(n_f * GROUP, BLOCK)

    query, key, value = (
        summed_part(j).astype(jnp.bfloat16).astype(jnp.float32) for j in range(3)
    )
    grad_z = summed_part(3)
    nothing = jnp.zeros((GROUP, BLOCK), jnp.float32)
    product = key * value
    before = jnp.concatenate([nothing, product[:-GROUP]], axis=0)
    conv = exact(product, band_here, (1, 0)) + exact(before, band_next, (1, 0))
    grad_query = grad_z * conv
    grad_conv = grad_z * query
    after = jnp.concatenate([grad_conv[GROUP:], nothing], axis=0)
    grad_product = exact(grad_conv, band_here, (1, 1)) + exact(after, band_next, (1, 1))
    for j, grad in enumerate((grad_query, grad_product * value, grad_product * key)):
        gp[:, j, mine, :] = grad.astype(jnp.bfloat16).reshape(n_f, GROUP, BLOCK)

    hops = (half_z, half_z - 1)
    needed = []
    for step in range(half_z):
        fresh = []
        for odd in range(2):
            for node in [odd + half_z - step] + ([odd - hops[DOWN] + step] if step < hops[DOWN] else []):
                off = (node // 2) % n_f
                if off not in fresh and all(off not in seen for seen in needed):
                    fresh.append(off)
        needed.append(fresh)
    if all(0 not in seen for seen in needed):
        needed[-1].append(0)

    def share(k, off, owner):
        rows = gp.at[tokens_at(off), :, group_rows(owner), :]
        return remote(rows, rows, ag_s.at[k - 1, off], ag_r.at[k - 1, off], peer(k), m)

    for fresh in needed:
        for off in fresh:
            for k in range(1, n_f):
                start(share(k, off, f))

    flip = (
        lax.broadcasted_iota(jnp.int32, (BLOCK, BLOCK), 0)
        + lax.broadcasted_iota(jnp.int32, (BLOCK, BLOCK), 1)
        == BLOCK - 1
    ).astype(jnp.float32)
    turned = exact(product, flip, (1, 0))
    corr = exact(turned, jnp.concatenate([grad_conv, after], axis=1), (0, 0))
    skewed = pltpu.roll(corr, 0, 1, stride=1, stride_axis=0)
    lags = pltpu.roll(jnp.sum(skewed, axis=0, keepdims=True), BLOCK + 1, 1)[:, :BLOCK]
    fg_all[f] = jnp.broadcast_to(lags * (1.0 / BLOCK), (8, BLOCK))

    def share_filter(k, owner):
        return remote(fg_all.at[owner], fg_all.at[owner], fg_s.at[k - 1], fg_r.at[k - 1], peer(k), m)

    def pair(off):
        chunks = pl.ds(2 * tokens_at(off), 2)
        return remote(pair_out.at[chunks], pair_in.at[chunks], pair_s.at[off], pair_r.at[off], f, other)

    def backward(off):
        for k in range(1, n_f):
            share(k, off, peer(n_f - k)).wait_recv()
        tb = tokens_at(off)
        grads = jnp.concatenate([gp[tb, j] for j in range(3)], axis=0)

        def rows_for(n, core):
            rows = pl.ds(pl.multiple_of((4 * n + 2 * core) * BLOCK, 2 * BLOCK), 2 * BLOCK)
            return dot(wn[rows, :], grads, (1, 0))

        for n in range(2):
            pair_out[2 * tb + n] = rows_for(n, 1 - c).astype(jnp.bfloat16)
        start(pair(off))
        for n in range(2):
            own[2 * tb + n] = rows_for(n, c)

    def pass_on(way, step, half):
        return remote(
            ring_out.at[way, step, half], ring_in.at[way, step, half],
            sum_s.at[way, step, half], sum_r.at[way, step, half], f, up if way == UP else down,
        )

    def local(slot, half):
        rows = slice(half * BLOCK, (half + 1) * BLOCK)
        return own[slot, rows, :] + pair_in[slot, rows, :].astype(jnp.float32)

    for off in needed[0]:
        backward(off)
    for step in range(half_z):
        for off in needed[step]:
            pair(off).wait_recv()
        for way in (UP, DOWN):
            if step < hops[way]:
                slot = along(half_z - step if way == UP else step - hops[DOWN])
                for half in range(2):
                    total = local(slot, half)
                    if step > 0:
                        pass_on(way, step - 1, half).wait_recv()
                        total = total + ring_in[way, step - 1, half].astype(jnp.float32)
                    ring_out[way, step, half] = total.astype(jnp.bfloat16)
                    start(pass_on(way, step, half))
        if step == 0:
            for k in range(1, n_f):
                start(share_filter(k, f))
        if step + 1 < half_z:
            for off in needed[step + 1]:
                backward(off)

    for half in range(2):
        total = local(z, half)
        for way in (UP, DOWN):
            pass_on(way, hops[way] - 1, half).wait_recv()
            total = total + ring_in[way, hops[way] - 1, half].astype(jnp.float32)
        last_out[half] = total.astype(jnp.bfloat16)
        start(remote(
            last_out.at[half], last_in.at[xh], last_s.at[half], last_r.at[xh], from_f, from_m(half)
        ))
    for k in range(1, n_f):
        share_filter(k, peer(n_f - k)).wait_recv()
    filter_grad[...] = jnp.concatenate([fg_all[g, 0:1, :] for g in range(n_f)], axis=0)
    for x in range(2):
        remote(last_out.at[x], last_in.at[x], last_s.at[x], last_r.at[x], to_f, to_m(x)).wait_recv()
    summed = last_in[0].astype(jnp.float32) + last_in[1].astype(jnp.float32)
    input_grad[...] = summed.T.astype(jnp.bfloat16)
    for copy in sent:
        copy.wait_send()


def on_device(n_f, n_z, tokens, in_values, in_scales, filters, out_weight, cotangent):
    channels = in_values.shape[2]
    features = PIECES * BLOCK
    bf16, f32 = jnp.bfloat16, jnp.float32
    dma = pltpu.SemaphoreType.DMA
    values, scales = in_values.transpose(1, 0, 2), in_scales.transpose(1, 0, 2)
    return pl.pallas_call(
        functools.partial(kernel, n_f, n_z),
        out_shape=(
            jax.ShapeDtypeStruct((BLOCK, BLOCK), bf16),
            jax.ShapeDtypeStruct((n_f, BLOCK), f32),
        ),
        in_specs=[pl.BlockSpec(memory_space=pl.ANY)] * 6,
        out_specs=(pl.BlockSpec(memory_space=pltpu.VMEM),) * 2,
        scratch_shapes=[
            pltpu.VMEM(values.shape, bf16),
            pltpu.VMEM(scales.shape, bf16),
            pltpu.VMEM(filters.shape, f32),
            pltpu.VMEM(out_weight.shape, bf16),
            pltpu.VMEM((n_z, 2, 2, 2, BLOCK, BLOCK), bf16),
            pltpu.VMEM((3 * channels, features), bf16),
            pltpu.VMEM((features, 3 * channels), bf16),
            pltpu.VMEM((channels, features), bf16),
            pltpu.VMEM((n_f, 4, channels, BLOCK), bf16),
            pltpu.VMEM((n_f - 1, n_f, 4, GROUP, BLOCK), bf16),
            pltpu.VMEM((n_f, 3, channels, BLOCK), bf16),
            pltpu.VMEM((n_f, 8, BLOCK), f32),
            pltpu.VMEM((n_z, 2 * BLOCK, BLOCK), f32),
            pltpu.VMEM((n_z, 2 * BLOCK, BLOCK), bf16),
            pltpu.VMEM((n_z, 2 * BLOCK, BLOCK), bf16),
            pltpu.VMEM((2, n_z // 2, 2, BLOCK, BLOCK), bf16),
            pltpu.VMEM((2, n_z // 2, 2, BLOCK, BLOCK), bf16),
            pltpu.VMEM((2, BLOCK, BLOCK), bf16),
            pltpu.VMEM((2, BLOCK, BLOCK), bf16),
            dma((4,)),
            dma((2,)), dma((2,)),
            dma((2, 2, n_z // 2)), dma((2, 2, n_z // 2)),
            dma((n_z,)), dma((n_z,)),
            dma((2, n_z)), dma((2, n_z)),
            dma((n_f - 1, n_f)), dma((n_f - 1, n_f)),
            dma((n_f - 1, n_f)), dma((n_f - 1, n_f)),
            dma((n_f - 1,)), dma((n_f - 1,)),
            dma((n_f,)), dma((n_f,)),
            dma((2, n_z // 2, 2)), dma((2, n_z // 2, 2)),
            dma((2,)), dma((2,)),
        ],
        compiler_params=pltpu.CompilerParams(
            collective_id=0, has_side_effects=True, vmem_limit_bytes=56 << 20
        ),
        name="hyena",
    )(tokens, cotangent, values, scales, filters, out_weight)


def solution(mesh):
    placed = (
        P("fsdp", "tensor"),
        P("fsdp", None, "tensor"),
        P("fsdp", None, "tensor"),
        P("tensor", None),
        P("tensor", "fsdp"),
        P("fsdp", "tensor"),
    )
    return jax.shard_map(
        functools.partial(on_device, mesh.shape["fsdp"], mesh.shape["tensor"] // 4),
        mesh=mesh,
        in_specs=placed,
        out_specs=(P("fsdp", "tensor"), P("tensor", None)),
        check_vma=False,
    )
```

time: 152 us -> 125 us (0.82)
  the two profiles are of different devices: /device:TPU:17 before, /device:TPU:9 now
where the time goes in v2:
time: 125 us
  Pallas kernels  122 us (98%)
  local copies, waits for them, and re-layouts  1.97 us (2%)
    pallas_call x1, Pallas kernels, on_device(): pl.pallas_call(functools.partial(kernel, n_f, n_z), out_shape=(jax.ShapeD...  122 us

profile of v2, /device:TPU:9, one launch (start us, length us, event | category | flops | bytes accessed | tf_op | source)
XLA Modules:
  0.0 124.9 jit_solution(16087701780024072647)
XLA Ops:
  0.6 122.3 %hyena.1 = (bf16[128,128]{1,0:T(8,128)(2,1)}, f32[8,128]{1,0:T(8,128)}) custom-call(bf16[128,128]{1,0:T(8,128)(2,1)} %tok.1, bf16[128,128]{1,0:T(8,128)(2,1)} %cot.1, bf16[3,1024,128]{2,1,0:T(8,128)(2,1)} %bitcast.2, bf16[3,8,128]{2,1,0:T(8,128)(2,1)} %bitcast.3, f32[8,128]{1,0:T(8,128)} %flt_hbm.1, bf16[128,1024]{1,0:T(8,128)(2,1)} %out_w_hbm.1), custom_call_target="tpu_custom_call" | custom-call | tf_op jit(solution)/shard_map/hyena/pallas_call | solution.py:332
  122.9 0.0 copy-start
  122.9 1.4 %copy.10 = bf16[128,128]{1,0:T(8,128)(2,1)} copy(bf16[128,128]{1,0:T(8,128)(2,1)} %get-tuple-element.4) | data formatting | bytes 65536
  124.3 0.0 copy-done
  124.3 0.6 copy.11
Async XLA Ops:
  122.9 1.4 %copy-start = (f32[8,128]{1,0:T(8,128)S(1)}, f32[8,128]{1,0:T(8,128)}, u32[]{:S(2)}) copy-start(f32[8,128]{1,0:T(8,128)} %get-tuple-element.5) | copy-start | bytes 12292

commit v3 on v2

--- a/solution.py
+++ b/solution.py
@@ -107,19 +107,26 @@
             wt[columns, rows] = scaled.T.astype(jnp.bfloat16)
         ow[:, rows] = out_w[:, piece * BLOCK : (piece + 1) * BLOCK]
 
-    steps = ((half_z, half_z - 1), (half_z - 1, half_z))
-
-    def ring(a, way, step, ahead=0):
+    steps = ((half_z, half_z - 1), (half_z - 1, half_z), (half_z, half_z - 1))
+
+    chains = ((0, xh), (1, xh), (0, 1 - xh))
+
+    def ring(chain, way, step, ahead=0):
         slot = along(-step - ahead if way == UP else step + ahead)
-        chunk = gathered.at[slot, c, xh, a]
+        a, half = chains[chain]
+        chunk = gathered.at[slot, c, half, a]
         return remote(
-            chunk, chunk, ring_s.at[a, way, step], ring_r.at[a, way, step],
+            chunk, chunk, ring_s.at[chain, way, step], ring_r.at[chain, way, step],
             f, up if way == UP else down,
         )
 
     def over_x(by, half):
-        chunk = gathered.at[along(by), c, half]
+        chunk = gathered.at[along(by), c, half, 1]
         return remote(chunk, chunk, slice_s.at[by % n_z], slice_r.at[by % n_z], f, across_x)
+
+    def first_over_x(half):
+        chunk = gathered.at[z, c, half, 0]
+        return remote(chunk, chunk, slice_s.at[n_z], slice_r.at[n_z], f, across_x)
 
     def over_core(by, half, which, core):
         chunk = gathered.at[along(by), core, half]
@@ -155,33 +162,45 @@
             for k in range(1, n_f):
                 start(scatter(k, off))
 
+    def arrived(chain, step):
+        for way in (UP, DOWN):
+            if step < steps[chain][way]:
+                ring(chain, way, step, 1).wait_recv()
+                if step + 1 < steps[chain][way]:
+                    start(ring(chain, way, step + 1))
+
     for a in range(2):
         block = gathered.at[z, c, xh, a]
         remote(block, block, perm_s.at[a], perm_r.at[a], f, other).wait_recv()
+        if a == 0:
+            start(first_over_x(xh))
         for way in (UP, DOWN):
             start(ring(a, way, 0))
     start(over_x(0, xh))
     start(over_core(0, xh, 0, c))
     done = 0
-    for step in range(half_z):
-        for a in range(2):
+    for step in range(half_z + 2):
+        if step < half_z:
+            for chain in range(2):
+                arrived(chain, step)
+            for by in nodes_at(step + 1):
+                start(over_x(by, xh))
+        if step == 0:
+            first_over_x(1 - xh).wait_recv()
             for way in (UP, DOWN):
-                if step < steps[a][way]:
-                    ring(a, way, step, 1).wait_recv()
-                    if step + 1 < steps[a][way]:
-                        start(ring(a, way, step + 1))
-        for by in nodes_at(step + 1):
-            start(over_x(by, xh))
-            start(over_core(by, xh, 0, c))
-        for by in nodes_at(step):
-            over_x(by, 1 - xh).wait_recv()
-            start(over_core(by, 1 - xh, 1, c))
-        if step == 2 * done + 2:
+                start(ring(2, way, 0))
+        if step >= 1:
+            if step - 1 < half_z:
+                arrived(2, step - 1)
+            for by in nodes_at(step - 1):
+                over_x(by, 1 - xh).wait_recv()
+                start(over_core(by, 1 - xh, 1, c))
+        if step < half_z:
+            for by in nodes_at(step + 1):
+                start(over_core(by, xh, 0, c))
+        if step >= 2 * done + 3 and done < half_f:
             products(done)
             done += 1
-    for by in nodes_at(half_z):
-        over_x(by, 1 - xh).wait_recv()
-        start(over_core(by, 1 - xh, 1, c))
     for distance in range(done, half_f + 1):
         products(distance)
 
@@ -359,8 +378,8 @@
             pltpu.VMEM((2, BLOCK, BLOCK), bf16),
             dma((4,)),
             dma((2,)), dma((2,)),
-            dma((2, 2, n_z // 2)), dma((2, 2, n_z // 2)),
-            dma((n_z,)), dma((n_z,)),
+            dma((3, 2, n_z // 2)), dma((3, 2, n_z // 2)),
+            dma((n_z + 1,)), dma((n_z + 1,)),
             dma((2, n_z)), dma((2, n_z)),
             dma((n_f - 1, n_f)), dma((n_f - 1, n_f)),
             dma((n_f - 1, n_f)), dma((n_f - 1, n_f)),

time: 125 us -> 121 us (0.968)
  Pallas kernels: 122 us -> 118 us
    pallas_call x1, Pallas kernels: 122 us -> 118 us  [on_device(): pl.pallas_call(functools.partial(kernel, n_f, n_z), out_shape=(jax.ShapeD...]
where the time goes in v3:
time: 121 us
  Pallas kernels  118 us (98%)
  local copies, waits for them, and re-layouts  1.97 us (2%)
    pallas_call x1, Pallas kernels, on_device(): pl.pallas_call(functools.partial(kernel, n_f, n_z), out_shape=(jax.ShapeD...  118 us

profile of v3, /device:TPU:9, one launch (start us, length us, event | category | flops | bytes accessed | tf_op | source)
XLA Modules:
  0.0 121.0 jit_solution(17907007755174634920)
XLA Ops:
  0.6 118.4 %hyena.1 = (bf16[128,128]{1,0:T(8,128)(2,1)}, f32[8,128]{1,0:T(8,128)}) custom-call(bf16[128,128]{1,0:T(8,128)(2,1)} %tok.1, bf16[128,128]{1,0:T(8,128)(2,1)} %cot.1, bf16[3,1024,128]{2,1,0:T(8,128)(2,1)} %bitcast.2, bf16[3,8,128]{2,1,0:T(8,128)(2,1)} %bitcast.3, f32[8,128]{1,0:T(8,128)} %flt_hbm.1, bf16[128,1024]{1,0:T(8,128)(2,1)} %out_w_hbm.1), custom_call_target="tpu_custom_call" | custom-call | tf_op jit(solution)/shard_map/hyena/pallas_call | solution.py:351
  119.1 0.0 copy-start
  119.1 1.4 %copy.10 = bf16[128,128]{1,0:T(8,128)(2,1)} copy(bf16[128,128]{1,0:T(8,128)(2,1)} %get-tuple-element.4) | data formatting | bytes 65536
  120.4 0.0 copy-done
  120.4 0.6 copy.11
Async XLA Ops:
  119.1 1.4 %copy-start = (f32[8,128]{1,0:T(8,128)S(1)}, f32[8,128]{1,0:T(8,128)}, u32[]{:S(2)}) copy-start(f32[8,128]{1,0:T(8,128)} %get-tuple-element.5) | copy-start | bytes 12292

commit v4 on v3

--- a/solution.py
+++ b/solution.py
@@ -44,8 +44,8 @@
     f, m = lax.axis_index("fsdp"), lax.axis_index("tensor")
     c, z, xh = lax.rem(m, 2), lax.rem(m // 2, n_z), m // (2 * n_z)
     along = lambda by: lax.rem(z + by + 2 * n_z, n_z)
-    up = (xh * n_z + along(1)) * 2 + c
-    down = (xh * n_z + along(-1)) * 2 + c
+    node = lambda by: (xh * n_z + along(by)) * 2 + c
+    up, down = node(1), node(-1)
     other = m + 1 - 2 * c
     across_x = ((1 - xh) * n_z + z) * 2 + c
     peer = lambda k: lax.rem(f + k, n_f)
@@ -57,6 +57,13 @@
     from_f = z // 2
     from_m = lambda half: PIECES * f + 4 * lax.rem(z, 2) + 2 * half + 1 - c
 
+    def parent(d):
+        if d % 3 < 2:
+            return d - 3 if d % 3 == 0 else d - 1
+        return d + 1 if d < half_z else d - 2
+
+    reach = sorted({abs(d - parent(d)) for d in range(1, half_z + 1)})
+
     def remote(src, dst, send, recv, fsdp, tensor):
         return pltpu.make_async_remote_copy(
             src_ref=src, dst_ref=dst, send_sem=send, recv_sem=recv,
@@ -78,7 +85,7 @@
     for load in loads:
         load.start()
     barrier = pltpu.get_barrier_semaphore()
-    greeted = [(f, up), (f, down), (f, other), (f, across_x)]
+    greeted = [(f, other), (f, across_x)] + [(f, node(way * by)) for by in reach for way in (1, -1)]
     greeted += [(peer(k), m) for k in range(1, n_f)]
     greeted += [(to_f, to_m(x)) for x in range(2)]
     greeted += [(from_f, from_m(h)) for h in range(2)]
@@ -234,24 +241,19 @@
     for j, grad in enumerate((grad_query, grad_product * value, grad_product * key)):
         gp[:, j, mine, :] = grad.astype(jnp.bfloat16).reshape(n_f, GROUP, BLOCK)
 
-    hops = (half_z, half_z - 1)
-    needed = []
-    for step in range(half_z):
-        fresh = []
-        for odd in range(2):
-            for node in [odd + half_z - step] + ([odd - hops[DOWN] + step] if step < hops[DOWN] else []):
-                off = (node // 2) % n_f
-                if off not in fresh and all(off not in seen for seen in needed):
-                    fresh.append(off)
-        needed.append(fresh)
-    if all(0 not in seen for seen in needed):
-        needed[-1].append(0)
+    tree = [d for d in (8, 7, 5, 4, 2, 6, 1, 3) if d <= half_z]
+    needed = {}
+    for d in tree + [0]:
+        needed[d] = []
+        for off in [((odd + by) // 2) % n_f for by in nodes_at(d) for odd in range(2)]:
+            if off not in needed[d] and all(off not in seen for seen in needed.values()):
+                needed[d].append(off)
 
     def share(k, off, owner):
         rows = gp.at[tokens_at(off), :, group_rows(owner), :]
         return remote(rows, rows, ag_s.at[k - 1, off], ag_r.at[k - 1, off], peer(k), m)
 
-    for fresh in needed:
+    for fresh in needed.values():
         for off in fresh:
             for k in range(1, n_f):
                 start(share(k, off, f))
@@ -290,43 +292,49 @@
         for n in range(2):
             own[2 * tb + n] = rows_for(n, c)
 
-    def pass_on(way, step, half):
+    def taken(half, way, d):
+        return d <= (half_z if (way == UP) == (half == 0) else half_z - 1)
+
+    def pass_on(half, way, d):
+        by = d - parent(d)
         return remote(
-            ring_out.at[way, step, half], ring_in.at[way, step, half],
-            sum_s.at[way, step, half], sum_r.at[way, step, half], f, up if way == UP else down,
-        )
+            ring_out.at[half, way, d - 1], ring_in.at[half, way, d - 1],
+            sum_s.at[half, way, d - 1], sum_r.at[half, way, d - 1], f, node(by if way == UP else -by),
+        )
+
+    def with_children(total, half, way, at):
+        for d in tree:
+            if parent(d) == at and taken(half, way, d):
+                pass_on(half, way, d).wait_recv()
+                total = total + ring_in[half, way, d - 1].astype(jnp.float32)
+        return total
 
     def local(slot, half):
         rows = slice(half * BLOCK, (half + 1) * BLOCK)
         return own[slot, rows, :] + pair_in[slot, rows, :].astype(jnp.float32)
 
+    for i, d in enumerate(tree):
+        for off in needed[d]:
+            backward(off)
+        for off in needed[d]:
+            pair(off).wait_recv()
+        for way in (UP, DOWN):
+            slot = along(d if way == UP else -d)
+            for half in range(2):
+                if taken(half, way, d):
+                    ring_out[half, way, d - 1] = with_children(local(slot, half), half, way, d).astype(jnp.bfloat16)
+                    start(pass_on(half, way, d))
+        if i == 0:
+            for k in range(1, n_f):
+                start(share_filter(k, f))
     for off in needed[0]:
         backward(off)
-    for step in range(half_z):
-        for off in needed[step]:
-            pair(off).wait_recv()
-        for way in (UP, DOWN):
-            if step < hops[way]:
-                slot = along(half_z - step if way == UP else step - hops[DOWN])
-                for half in range(2):
-                    total = local(slot, half)
-                    if step > 0:
-                        pass_on(way, step - 1, half).wait_recv()
-                        total = total + ring_in[way, step - 1, half].astype(jnp.float32)
-                    ring_out[way, step, half] = total.astype(jnp.bfloat16)
-                    start(pass_on(way, step, half))
-        if step == 0:
-            for k in range(1, n_f):
-                start(share_filter(k, f))
-        if step + 1 < half_z:
-            for off in needed[step + 1]:
-                backward(off)
+        pair(off).wait_recv()
 
     for half in range(2):
         total = local(z, half)
         for way in (UP, DOWN):
-            pass_on(way, hops[way] - 1, half).wait_recv()
-            total = total + ring_in[way, hops[way] - 1, half].astype(jnp.float32)
+            total = with_children(total, half, way, 0)
         last_out[half] = total.astype(jnp.bfloat16)
         start(remote(
             last_out.at[half], last_in.at[xh], last_s.at[half], last_r.at[xh], from_f, from_m(half)
@@ -372,8 +380,8 @@
             pltpu.VMEM((n_z, 2 * BLOCK, BLOCK), f32),
             pltpu.VMEM((n_z, 2 * BLOCK, BLOCK), bf16),
             pltpu.VMEM((n_z, 2 * BLOCK, BLOCK), bf16),
-            pltpu.VMEM((2, n_z // 2, 2, BLOCK, BLOCK), bf16),
-            pltpu.VMEM((2, n_z // 2, 2, BLOCK, BLOCK), bf16),
+            pltpu.VMEM((2, 2, n_z // 2, BLOCK, BLOCK), bf16),
+            pltpu.VMEM((2, 2, n_z // 2, BLOCK, BLOCK), bf16),
             pltpu.VMEM((2, BLOCK, BLOCK), bf16),
             pltpu.VMEM((2, BLOCK, BLOCK), bf16),
             dma((4,)),
@@ -385,7 +393,7 @@
             dma((n_f - 1, n_f)), dma((n_f - 1, n_f)),
             dma((n_f - 1,)), dma((n_f - 1,)),
             dma((n_f,)), dma((n_f,)),
-            dma((2, n_z // 2, 2)), dma((2, n_z // 2, 2)),
+            dma((2, 2, n_z // 2)), dma((2, 2, n_z // 2)),
             dma((2,)), dma((2,)),
         ],
         compiler_params=pltpu.CompilerParams(

time: 121 us -> 117 us (0.967)
  Pallas kernels: 118 us -> 114 us
    pallas_call x1, Pallas kernels: 118 us -> 114 us  [on_device(): pl.pallas_call(functools.partial(kernel, n_f, n_z), out_shape=(jax.ShapeD...]
where the time goes in v4:
time: 117 us
  Pallas kernels  114 us (97%)
  local copies, waits for them, and re-layouts  1.97 us (2%)
    pallas_call x1, Pallas kernels, on_device(): pl.pallas_call(functools.partial(kernel, n_f, n_z), out_shape=(jax.ShapeD...  114 us

profile of v4, /device:TPU:9, one launch (start us, length us, event | category | flops | bytes accessed | tf_op | source)
XLA Modules:
  0.0 116.7 jit_solution(18422143372487090393)
XLA Ops:
  0.6 114.1 %hyena.1 = (bf16[128,128]{1,0:T(8,128)(2,1)}, f32[8,128]{1,0:T(8,128)}) custom-call(bf16[128,128]{1,0:T(8,128)(2,1)} %tok.1, bf16[128,128]{1,0:T(8,128)(2,1)} %cot.1, bf16[3,1024,128]{2,1,0:T(8,128)(2,1)} %bitcast.2, bf16[3,8,128]{2,1,0:T(8,128)(2,1)} %bitcast.3, f32[8,128]{1,0:T(8,128)} %flt_hbm.1, bf16[128,1024]{1,0:T(8,128)(2,1)} %out_w_hbm.1), custom_call_target="tpu_custom_call" | custom-call | tf_op jit(solution)/shard_map/hyena/pallas_call | solution.py:359
  114.8 0.0 copy-start
  114.8 1.4 %copy.10 = bf16[128,128]{1,0:T(8,128)(2,1)} copy(bf16[128,128]{1,0:T(8,128)(2,1)} %get-tuple-element.4) | data formatting | bytes 65536
  116.1 0.0 copy-done
  116.2 0.6 copy.11
Async XLA Ops:
  114.8 1.4 %copy-start = (f32[8,128]{1,0:T(8,128)S(1)}, f32[8,128]{1,0:T(8,128)}, u32[]{:S(2)}) copy-start(f32[8,128]{1,0:T(8,128)} %get-tuple-element.5) | copy-start | bytes 12292

commit v5 on v4

--- a/solution.py
+++ b/solution.py
@@ -342,11 +342,13 @@
     for k in range(1, n_f):
         share_filter(k, peer(n_f - k)).wait_recv()
     filter_grad[...] = jnp.concatenate([fg_all[g, 0:1, :] for g in range(n_f)], axis=0)
+    for copy in sent[:-2]:
+        copy.wait_send()
     for x in range(2):
         remote(last_out.at[x], last_in.at[x], last_s.at[x], last_r.at[x], to_f, to_m(x)).wait_recv()
     summed = last_in[0].astype(jnp.float32) + last_in[1].astype(jnp.float32)
     input_grad[...] = summed.T.astype(jnp.bfloat16)
-    for copy in sent:
+    for copy in sent[-2:]:
         copy.wait_send()
 
 

time: 117 us -> 117 us (level)
  no operation moved by 1% of the time
where the time goes in v5:
time: 117 us; the launch traced here: 116 us
  Pallas kernels  114 us (97%)
  local copies, waits for them, and re-layouts  1.97 us (2%)
    pallas_call x1, Pallas kernels, on_device(): pl.pallas_call(functools.partial(kernel, n_f, n_z), out_shape=(jax.ShapeD...  114 us

profile of v5, /device:TPU:9, one launch (start us, length us, event | category | flops | bytes accessed | tf_op | source)
XLA Modules:
  0.0 116.3 jit_solution(13947707727331872605)
XLA Ops:
  0.6 113.7 %hyena.1 = (bf16[128,128]{1,0:T(8,128)(2,1)}, f32[8,128]{1,0:T(8,128)}) custom-call(bf16[128,128]{1,0:T(8,128)(2,1)} %tok.1, bf16[128,128]{1,0:T(8,128)(2,1)} %cot.1, bf16[3,1024,128]{2,1,0:T(8,128)(2,1)} %bitcast.2, bf16[3,8,128]{2,1,0:T(8,128)(2,1)} %bitcast.3, f32[8,128]{1,0:T(8,128)} %flt_hbm.1, bf16[128,1024]{1,0:T(8,128)(2,1)} %out_w_hbm.1), custom_call_target="tpu_custom_call" | custom-call | tf_op jit(solution)/shard_map/hyena/pallas_call | solution.py:361
  114.4 0.0 copy-start
  114.4 1.4 %copy.10 = bf16[128,128]{1,0:T(8,128)(2,1)} copy(bf16[128,128]{1,0:T(8,128)(2,1)} %get-tuple-element.4) | data formatting | bytes 65536
  115.7 0.0 copy-done
  115.8 0.6 copy.11
Async XLA Ops:
  114.4 1.4 %copy-start = (f32[8,128]{1,0:T(8,128)S(1)}, f32[8,128]{1,0:T(8,128)}, u32[]{:S(2)}) copy-start(f32[8,128]{1,0:T(8,128)} %get-tuple-element.5) | copy-start | bytes 12292

commit v6 on v5

--- a/solution.py
+++ b/solution.py
@@ -85,10 +85,9 @@
     for load in loads:
         load.start()
     barrier = pltpu.get_barrier_semaphore()
-    greeted = [(f, other), (f, across_x)] + [(f, node(way * by)) for by in reach for way in (1, -1)]
+    greeted = [(to_f, to_m(x)) for x in range(2)] + [(from_f, from_m(h)) for h in range(2)]
     greeted += [(peer(k), m) for k in range(1, n_f)]
-    greeted += [(to_f, to_m(x)) for x in range(2)]
-    greeted += [(from_f, from_m(h)) for h in range(2)]
+    greeted += [(f, other), (f, across_x)] + [(f, node(way * by)) for by in reach for way in (1, -1)]
     for fsdp, tensor in greeted:
         pl.semaphore_signal(
             barrier, inc=1, device_id={"fsdp": fsdp, "tensor": tensor}, device_id_type=MESH
@@ -258,16 +257,17 @@
             for k in range(1, n_f):
                 start(share(k, off, f))
 
-    flip = (
-        lax.broadcasted_iota(jnp.int32, (BLOCK, BLOCK), 0)
-        + lax.broadcasted_iota(jnp.int32, (BLOCK, BLOCK), 1)
-        == BLOCK - 1
-    ).astype(jnp.float32)
-    turned = exact(product, flip, (1, 0))
-    corr = exact(turned, jnp.concatenate([grad_conv, after], axis=1), (0, 0))
-    skewed = pltpu.roll(corr, 0, 1, stride=1, stride_axis=0)
-    lags = pltpu.roll(jnp.sum(skewed, axis=0, keepdims=True), BLOCK + 1, 1)[:, :BLOCK]
-    fg_all[f] = jnp.broadcast_to(lags * (1.0 / BLOCK), (8, BLOCK))
+    def filter_sums():
+        flip = (
+            lax.broadcasted_iota(jnp.int32, (BLOCK, BLOCK), 0)
+            + lax.broadcasted_iota(jnp.int32, (BLOCK, BLOCK), 1)
+            == BLOCK - 1
+        ).astype(jnp.float32)
+        turned = exact(product, flip, (1, 0))
+        corr = exact(turned, jnp.concatenate([grad_conv, after], axis=1), (0, 0))
+        skewed = pltpu.roll(corr, 0, 1, stride=1, stride_axis=0)
+        lags = pltpu.roll(jnp.sum(skewed, axis=0, keepdims=True), BLOCK + 1, 1)[:, :BLOCK]
+        fg_all[f] = jnp.broadcast_to(lags * (1.0 / BLOCK), (8, BLOCK))
 
     def share_filter(k, owner):
         return remote(fg_all.at[owner], fg_all.at[owner], fg_s.at[k - 1], fg_r.at[k - 1], peer(k), m)
@@ -313,7 +313,7 @@
         rows = slice(half * BLOCK, (half + 1) * BLOCK)
         return own[slot, rows, :] + pair_in[slot, rows, :].astype(jnp.float32)
 
-    for i, d in enumerate(tree):
+    for d in tree:
         for off in needed[d]:
             backward(off)
         for off in needed[d]:
@@ -324,7 +324,8 @@
                 if taken(half, way, d):
                     ring_out[half, way, d - 1] = with_children(local(slot, half), half, way, d).astype(jnp.bfloat16)
                     start(pass_on(half, way, d))
-        if i == 0:
+        if d == 2:
+            filter_sums()
             for k in range(1, n_f):
                 start(share_filter(k, f))
     for off in needed[0]:

time: 117 us -> 116 us (level)
  no operation moved by 1% of the time
where the time goes in v6:
time: 116 us
  Pallas kernels  114 us (98%)
  local copies, waits for them, and re-layouts  1.97 us (2%)
    pallas_call x1, Pallas kernels, on_device(): pl.pallas_call(functools.partial(kernel, n_f, n_z), out_shape=(jax.ShapeD...  114 us

profile of v6, /device:TPU:9, one launch (start us, length us, event | category | flops | bytes accessed | tf_op | source)
XLA Modules:
  0.0 116.3 jit_solution(15012250846471691527)
XLA Ops:
  0.6 113.7 %hyena.1 = (bf16[128,128]{1,0:T(8,128)(2,1)}, f32[8,128]{1,0:T(8,128)}) custom-call(bf16[128,128]{1,0:T(8,128)(2,1)} %tok.1, bf16[128,128]{1,0:T(8,128)(2,1)} %cot.1, bf16[3,1024,128]{2,1,0:T(8,128)(2,1)} %bitcast.2, bf16[3,8,128]{2,1,0:T(8,128)(2,1)} %bitcast.3, f32[8,128]{1,0:T(8,128)} %flt_hbm.1, bf16[128,1024]{1,0:T(8,128)(2,1)} %out_w_hbm.1), custom_call_target="tpu_custom_call" | custom-call | tf_op jit(solution)/shard_map/hyena/pallas_call | solution.py:362
  114.3 0.0 copy-start
  114.3 1.4 %copy.10 = bf16[128,128]{1,0:T(8,128)(2,1)} copy(bf16[128,128]{1,0:T(8,128)(2,1)} %get-tuple-element.4) | data formatting | bytes 65536
  115.7 0.0 copy-done
  115.7 0.6 copy.11
Async XLA Ops:
  114.3 1.4 %copy-start = (f32[8,128]{1,0:T(8,128)S(1)}, f32[8,128]{1,0:T(8,128)}, u32[]{:S(2)}) copy-start(f32[8,128]{1,0:T(8,128)} %get-tuple-element.5) | copy-start | bytes 12292
